TPU v7x, 32 devices: a whole 2x2x4 slice. The times are simulated.
32 devices in a mesh: tok: 4 (over y, core), feat: 8 (over z, x).
Axes of the slice: x: 2, y: 2, z: 4, core: 2. Of those that a mesh axis runs over, the one named last changes fastest.
Arguments:
- tokens: bfloat16 [4096, 2048], P('tok', 'feat'), may hold values from -6 to 6
- level_bits: int32 [2, 4], replicated, may hold values from 0 to 3, each once within a row
- up_blocks: bfloat16 [2, 16, 5, 128, 512], P(None, 'feat', None, None, 'tok'), may hold values from -0.21875 to 0.21875
- down_blocks: bfloat16 [2, 16, 5, 512, 128], P(None, 'feat', None, None, 'tok'), may hold values from -0.109375 to 0.109375
- rank_in: bfloat16 [2, 2048, 256], replicated, may hold values from -0.125 to 0.125
- rank_up: bfloat16 [2, 256, 8192], P(None, None, 'feat'), may hold values from -0.15625 to 0.15625
- rank_down: bfloat16 [2, 8192, 256], P(None, 'feat'), may hold values from -0.0625 to 0.0625
- rank_out: bfloat16 [2, 256, 2048], P(None, None, 'feat'), may hold values from -0.15625 to 0.15625
Outputs:
- outputs: bfloat16 [4096, 2048], P('tok', 'feat')
Inputs may be any that keep to these rules, and one draw needn't show every extreme that they name: `level_bits`: each row is a permutation of the bits 0 to 3.
All inputs are finite; a program needn't handle non-finite values.
Results may differ from a plain program's by a relative error of at most 0.015.
Values may be sent and summed in bfloat16 or wider, within the bound.
A program may use at most 64 MiB of HBM per device.

v0:
```python
import jax
import jax.numpy as jnp
from jax import lax
from jax.sharding import PartitionSpec as P

D = 2048
HID = 8192
NB = 16
LAYERS = 2


def from_partner(value, axis, distance):
    return lax.ppermute(value, axis, [(i, i ^ 1 << distance) for i in range(lax.axis_size(axis))])


def flip_pairs(array, axis, bit_num):
    shape = array.shape
    stride = 1 << bit_num
    count = shape[axis]
    split = shape[:axis] + (count // (2 * stride), 2, stride) + shape[axis + 1 :]
    return jnp.flip(array.reshape(split), axis + 1).reshape(shape)


def block_product(left, right):
    return jnp.einsum("tjd,jdh->tjh", left, right, preferred_element_type=jnp.float32)


def level_weight(weights, bits_row, bit_num):
    level_num = jnp.sum(
        jnp.where(bits_row == bit_num, jnp.arange(bits_row.shape[0], dtype=jnp.int32), 0)
    )
    return lax.dynamic_index_in_dim(weights, 1 + level_num, 1, keepdims=False)


def per_device(tokens, level_bits, up_blocks, down_blocks, rank_in, rank_up, rank_down, rank_out):
    width_block = D // NB
    hidden_block = HID // NB
    local_width = tokens.shape[1]
    local_blocks = local_width // width_block
    local_bits = local_blocks.bit_length() - 1
    all_bits = NB.bit_length() - 1
    rows = tokens.shape[0]
    my_index = lax.axis_index("feat")
    current = tokens
    for layer_num in range(LAYERS):
        bits_row = level_bits[layer_num]
        up_whole, down_whole = (
            lax.all_gather(up_blocks[layer_num], "tok", axis=3, tiled=True),
            lax.all_gather(down_blocks[layer_num], "tok", axis=3, tiled=True),
        )
        blocked = current.reshape(rows, local_blocks, width_block)
        pre_act = block_product(blocked, up_whole[:, 0])
        for bit_num in range(all_bits):
            if bit_num < local_bits:
                partner = flip_pairs(blocked, 1, bit_num)
            else:
                partner = from_partner(blocked, "feat", bit_num - local_bits)
            pre_act = pre_act + block_product(partner, level_weight(up_whole, bits_row, bit_num))
        rows_in = lax.dynamic_slice_in_dim(
            rank_in[layer_num], my_index * local_width, local_width, 0
        )
        partial_latent = jnp.dot(current, rows_in, preferred_element_type=jnp.float32)
        latent = lax.psum(partial_latent.astype(jnp.bfloat16), "feat")
        pre_act = pre_act + jnp.dot(
            latent, rank_up[layer_num], preferred_element_type=jnp.float32
        ).reshape(rows, local_blocks, hidden_block)
        hidden = jax.nn.gelu(pre_act, approximate=False).astype(jnp.bfloat16)
        partial_back = jnp.dot(
            hidden.reshape(rows, -1), rank_down[layer_num], preferred_element_type=jnp.float32
        )
        latent_back = lax.psum(partial_back.astype(jnp.bfloat16), "feat")
        result = jnp.dot(
            latent_back, rank_out[layer_num], preferred_element_type=jnp.float32
        ).reshape(rows, local_blocks, width_block)
        result = result + block_product(hidden, down_whole[:, 0])
        for bit_num in range(all_bits):
            weight = level_weight(down_whole, bits_row, bit_num)
            term = block_product(hidden, weight)
            if bit_num < local_bits:
                term = flip_pairs(term, 1, bit_num)
            else:
                term = from_partner(term.astype(jnp.bfloat16), "feat", bit_num - local_bits).astype(
                    term.dtype
                )
            result = result + term
        current = (current.astype(jnp.float32) + result.reshape(rows, -1)).astype(jnp.bfloat16)
    return current


def solution(mesh):
    return jax.shard_map(
        per_device,
        mesh=mesh,
        in_specs=(
            P("tok", "feat"),
            P(),
            P(None, "feat", None, None, "tok"),
            P(None, "feat", None, None, "tok"),
            P(),
            P(None, None, "feat"),
            P(None, "feat", None),
            P(None, None, "feat"),
        ),
        out_specs=P("tok", "feat"),
        check_vma=False,
    )
```

profile of v0, /device:TPU:0, one launch (start us, length us, event | category | flops | bytes accessed | tf_op | source)
XLA Modules:
  0.0 430.5 jit_solution(16556435466339181507)
XLA Ops:
  7.4 2.7 fusion.123
  15.4 4.1 collective-permute-start.2
  32.5 70.6 %all-reduce.5.cloned.1.call-done = bf16[1024,256]{1,0:T(8,128)(2,1)} async-done(((bf16[1024,256]{1,0:T(8,128)(2,1)}), bf16[1024,256]{1,0:T(8,128)(2,1)}) %all-reduce.5.cloned.1.call-update) | async-done | bytes 524304 | tf_op jit(solution)/shard_map/psum | solution.py:63
  103.1 3.7 fusion.46
  112.8 7.0 %fusion.32 = (u8[1024,512]{0,1:T(8,128)(4,1)}, u8[1024,512]{0,1:T(8,128)(4,1)}, f32[1024,2,512]{0,2,1:T(8,128)}) fusion(f32[1024,2,512]{0,2,1:T(8,128)S(1)} %copy-done, bf16[1024,2,128]{2,0,1:T(8,128)(2,1)} %collective-permute-done.2, bf16[1,2,5,128,512]{3,4,1,2,0:T(8,128)(2,1)} %all-gather.9.cloned.1.call-done, s32[]{:T(128)S(6)} %select_n.78, ...), kind=kOutput, calls=%fused_computation.82 | convolution fusion | flops 286261248 | bytes 27000836 | tf_op jit(solution)/shard_map/tjd,jdh->tjh/dot_general | solution.py:25
  119.7 11.0 %fusion.2 = bf16[1024,2,512]{0,2,1:T(8,128)(2,1)S(1)} fusion(f32[1024,2,512]{0,2,1:T(8,128)} %get-tuple-element.27, u8[1024,512]{0,1:T(8,128)(4,1)} %get-tuple-element.8, u8[1024,512]{0,1:T(8,128)(4,1)} %get-tuple-element.7), kind=kLoop, calls=%fused_computation.4 | loop fusion | flops 73400320 | bytes 7340032 | tf_op jit(solution)/shard_map/convert_element_type | solution.py:67
  146.6 2.5 convolution_bitcast_fusion.1
  149.1 17.2 %collective-permute-done.5 = bf16[1024,2,128]{0,2,1:T(8,128)(2,1)} collective-permute-done((bf16[1024,2,128]{0,2,1:T(8,128)(2,1)}, bf16[1024,2,128]{0,2,1:T(8,128)(2,1)}, u32[]{:S(2)}, u32[]{:S(2)}) %collective-permute-start.5) | collective-permute-done | bytes 524320 | tf_op jit(solution)/shard_map/ppermute | solution.py:13
  166.7 54.3 %all-reduce.7.cloned.1.call-done = bf16[1024,256]{1,0:T(8,128)(2,1)} async-done(((bf16[1024,256]{1,0:T(8,128)(2,1)}), bf16[1024,256]{1,0:T(8,128)(2,1)}) %all-reduce.7.cloned.1.call-update) | async-done | bytes 524304 | tf_op jit(solution)/shard_map/psum | solution.py:71
  221.1 2.7 convert_add_fusion.1
  237.3 3.7 fusion.52
  241.0 2.6 fusion.40
  243.6 15.6 %collective-permute-done.7 = bf16[1024,2,128]{2,0,1:T(8,128)(2,1)} collective-permute-done((bf16[1024,2,128]{2,0,1:T(8,128)(2,1)}, bf16[1024,2,128]{2,0,1:T(8,128)(2,1)}, u32[]{:S(2)}, u32[]{:S(2)}) %collective-permute-start.7) | collective-permute-done | bytes 524320 | tf_op jit(solution)/shard_map/ppermute | solution.py:13
  259.3 3.7 fusion.59
  263.0 3.7 fusion.61
  266.7 43.1 %all-reduce.9.cloned.1.call-done = bf16[1024,256]{1,0:T(8,128)(2,1)} async-done(((bf16[1024,256]{1,0:T(8,128)(2,1)}), bf16[1024,256]{1,0:T(8,128)(2,1)}) %all-reduce.9.cloned.1.call-update) | async-done | bytes 524304 | tf_op jit(solution)/shard_map/psum | solution.py:63
  312.2 6.9 %fusion.33 = (u8[1024,512]{0,1:T(8,128)(4,1)S(1)}, u8[1024,512]{0,1:T(8,128)(4,1)S(1)}, f32[1024,2,512]{0,2,1:T(8,128)S(1)}) fusion(f32[1024,2,512]{0,2,1:T(8,128)S(1)} %fusion.38, bf16[1024,2,128]{2,0,1:T(8,128)(2,1)S(1)} %collective-permute-done.8, bf16[1,2,5,128,512]{3,4,1,2,0:T(8,128)(2,1)S(1)} %copy-done.7, s32[]{:T(128)S(6)} %select_n.87, ...), kind=kOutput, calls=%fused_computation.83 | convolution fusion | flops 286261248 | bytes 27000836 | tf_op jit(solution)/shard_map/tjd,jdh->tjh/dot_general | solution.py:25
  319.1 9.6 %fusion.5 = bf16[1024,2,512]{0,2,1:T(8,128)(2,1)S(1)} fusion(f32[1024,2,512]{0,2,1:T(8,128)S(1)} %get-tuple-element.28, u8[1024,512]{0,1:T(8,128)(4,1)S(1)} %get-tuple-element.6, u8[1024,512]{0,1:T(8,128)(4,1)S(1)} %get-tuple-element.5), kind=kLoop, calls=%fused_computation.7 | loop fusion | flops 73400320 | bytes 7340032 | tf_op jit(solution)/shard_map/convert_element_type | solution.py:67
  339.9 2.4 convolution_bitcast_fusion.2
  344.7 2.4 convolution_bitcast_fusion
  347.1 11.0 %collective-permute-done.11 = bf16[1024,2,128]{0,2,1:T(8,128)(2,1)} collective-permute-done((bf16[1024,2,128]{0,2,1:T(8,128)(2,1)S(1)}, bf16[1024,2,128]{0,2,1:T(8,128)(2,1)}, u32[]{:S(2)}, u32[]{:S(2)}) %collective-permute-start.11) | collective-permute-done | bytes 524320 | tf_op jit(solution)/shard_map/ppermute | solution.py:13
  358.1 3.3 collective-permute-done.10
  361.3 58.0 %all-reduce.11.cloned.1.call-done = bf16[1024,256]{1,0:T(8,128)(2,1)} async-done(((bf16[1024,256]{1,0:T(8,128)(2,1)}), bf16[1024,256]{1,0:T(8,128)(2,1)}) %all-reduce.11.cloned.1.call-update) | async-done | bytes 524304 | tf_op jit(solution)/shard_map/psum | solution.py:71
  419.4 2.7 convert_add_fusion
  (113 shorter events, 60.7 us)
Async XLA Ops:
  7.4 95.7 %all-reduce.5.cloned.1.call-start = ((), (), s32[]{:S(2)}) async-start(), calls=%async_computation | async-start | bytes 1048576 | tf_op jit(solution)/shard_map/psum | solution.py:63
  10.1 15.2 %copy-start.13 = (s32[2,4]{1,0:T(2,128)S(1)}, s32[2,4]{1,0:T(2,128)}, u32[]{:S(2)}) copy-start(s32[2,4]{1,0:T(2,128)} %param.9) | copy-start | bytes 100
  11.2 20.0 %copy-start.11 = (bf16[2,256,1024]{2,1,0:T(8,128)(2,1)S(1)}, bf16[2,256,1024]{2,1,0:T(8,128)(2,1)}, u32[]{:S(2)}) copy-start(bf16[2,256,1024]{2,1,0:T(8,128)(2,1)} %param.13) | copy-start | bytes 3145732
  11.2 95.6 %all-gather.9.cloned.1.call-start = ((), (), s32[]{:S(2)}) async-start(), calls=%async_computation.4 | async-start | bytes 1638400 | tf_op jit(solution)/shard_map/all_gather | solution.py:48
  14.2 119.7 %all-gather.11.cloned.1.call-start = ((), (), s32[]{:S(2)}) async-start(), calls=%async_computation.5 | async-start | bytes 1638400 | tf_op jit(solution)/shard_map/all_gather | solution.py:49
  14.4 18.0 %copy-start.2 = (bf16[1024,256]{0,1:T(8,128)(2,1)}, bf16[1024,256]{0,1:T(8,128)(2,1)S(1)}, u32[]{:S(2)}) copy-start(bf16[1024,256]{0,1:T(8,128)(2,1)S(1)} %copy.31) | copy-start | bytes 1572868
  15.4 96.6 %collective-permute-start.2 = (bf16[1024,2,128]{2,0,1:T(8,128)(2,1)}, bf16[1024,2,128]{2,0,1:T(8,128)(2,1)}, u32[]{:S(2)}, u32[]{:S(2)}) collective-permute-start(bf16[1024,2,128]{2,0,1:T(8,128)(2,1)} %copy.36), channel_id=1, source_target_pairs={{0,4},{1,5},{2,6},{3,7},{4,0},{5,1},{6,2},{7,3},{8,12},{9,13},{10,... | collective-permute-start | bytes 1572872 | tf_op jit(solution)/shard_map/ppermute | solution.py:13
  19.5 87.3 %collective-permute-start.1 = (bf16[1024,2,128]{2,0,1:T(8,128)(2,1)}, bf16[1024,2,128]{2,0,1:T(8,128)(2,1)}, u32[]{:S(2)}, u32[]{:S(2)}) collective-permute-start(bf16[1024,2,128]{2,0,1:T(8,128)(2,1)} %copy.36), channel_id=1, source_target_pairs={{0,2},{1,3},{2,0},{3,1},{4,6},{5,7},{6,4},{7,5},{8,10},{9,11},{10,... | collective-permute-start | bytes 1572872 | tf_op jit(solution)/shard_map/ppermute | solution.py:13
  21.1 87.7 %collective-permute-start = (bf16[1024,2,128]{2,0,1:T(8,128)(2,1)}, bf16[1024,2,128]{2,0,1:T(8,128)(2,1)}, u32[]{:S(2)}, u32[]{:S(2)}) collective-permute-start(bf16[1024,2,128]{2,0,1:T(8,128)(2,1)} %copy.36), channel_id=1, source_target_pairs={{0,1},{1,0},{2,3},{3,2},{4,5},{5,4},{6,7},{7,6},{8,9},{9,8},{10,11... | collective-permute-start | bytes 1572872 | tf_op jit(solution)/shard_map/ppermute | solution.py:13
  25.2 195.8 %all-reduce.7.cloned.1.call-start = ((), (), s32[]{:S(2)}) async-start(), calls=%async_computation.1 | async-start | bytes 1048576 | tf_op jit(solution)/shard_map/psum | solution.py:71
  132.4 104.9 %all-gather.13.cloned.1.call-start = ((), (), s32[]{:S(2)}) async-start(), calls=%async_computation.6 | async-start | bytes 1638400 | tf_op jit(solution)/shard_map/all_gather | solution.py:48
  133.6 176.2 %all-reduce.9.cloned.1.call-start = ((), (), s32[]{:S(2)}) async-start(), calls=%async_computation.2 | async-start | bytes 1048576 | tf_op jit(solution)/shard_map/psum | solution.py:63
  136.1 30.2 %collective-permute-start.5 = (bf16[1024,2,128]{0,2,1:T(8,128)(2,1)}, bf16[1024,2,128]{0,2,1:T(8,128)(2,1)}, u32[]{:S(2)}, u32[]{:S(2)}) collective-permute-start(bf16[1024,2,128]{0,2,1:T(8,128)(2,1)} %fusion.23), channel_id=1, source_target_pairs={{0,4},{1,5},{2,6},{3,7},{4,0},{5,1},{6,2},{7,3},{8,12},{9,13},{10,... | collective-permute-start | bytes 1572872 | tf_op jit(solution)/shard_map/ppermute | solution.py:13
  139.8 26.9 %collective-permute-start.4 = (bf16[1024,2,128]{0,2,1:T(8,128)(2,1)}, bf16[1024,2,128]{0,2,1:T(8,128)(2,1)}, u32[]{:S(2)}, u32[]{:S(2)}) collective-permute-start(bf16[1024,2,128]{0,2,1:T(8,128)(2,1)} %fusion.22), channel_id=1, source_target_pairs={{0,2},{1,3},{2,0},{3,1},{4,6},{5,7},{6,4},{7,5},{8,10},{9,11},{10,... | collective-permute-start | bytes 1572872 | tf_op jit(solution)/shard_map/ppermute | solution.py:13
  143.3 23.4 %collective-permute-start.3 = (bf16[1024,2,128]{0,2,1:T(8,128)(2,1)}, bf16[1024,2,128]{0,2,1:T(8,128)(2,1)}, u32[]{:S(2)}, u32[]{:S(2)}) collective-permute-start(bf16[1024,2,128]{0,2,1:T(8,128)(2,1)} %fusion.21), channel_id=1, source_target_pairs={{0,1},{1,0},{2,3},{3,2},{4,5},{5,4},{6,7},{7,6},{8,9},{9,8},{10,11... | collective-permute-start | bytes 1572872 | tf_op jit(solution)/shard_map/ppermute | solution.py:13
  146.6 77.2 %copy-start.4 = (bf16[1024,256]{0,1:T(8,128)(2,1)S(1)}, bf16[1024,256]{0,1:T(8,128)(2,1)}, u32[]{:S(2)}) copy-start(bf16[1024,256]{0,1:T(8,128)(2,1)} %copy-done.2) | copy-start | bytes 1572868
  226.0 102.7 %all-gather.15.cloned.1.call-start = ((), (), s32[]{:S(2)}) async-start(), calls=%async_computation.7 | async-start | bytes 1638400 | tf_op jit(solution)/shard_map/all_gather | solution.py:49
  226.9 192.5 %all-reduce.11.cloned.1.call-start = ((), (), s32[]{:S(2)}) async-start(), calls=%async_computation.3 | async-start | bytes 1048576 | tf_op jit(solution)/shard_map/psum | solution.py:71
  233.3 78.5 %collective-permute-start.8 = (bf16[1024,2,128]{2,0,1:T(8,128)(2,1)}, bf16[1024,2,128]{2,0,1:T(8,128)(2,1)S(1)}, u32[]{:S(2)}, u32[]{:S(2)}) collective-permute-start(bf16[1024,2,128]{2,0,1:T(8,128)(2,1)} %copy.50), channel_id=1, source_target_pairs={{0,4},{1,5},{2,6},{3,7},{4,0},{5,1},{6,2},{7,3},{8,12},{9,13},{10,... | collective-permute-start | bytes 1572872 | tf_op jit(solution)/shard_map/ppermute | solution.py:13
  234.8 24.4 %collective-permute-start.7 = (bf16[1024,2,128]{2,0,1:T(8,128)(2,1)}, bf16[1024,2,128]{2,0,1:T(8,128)(2,1)}, u32[]{:S(2)}, u32[]{:S(2)}) collective-permute-start(bf16[1024,2,128]{2,0,1:T(8,128)(2,1)} %copy.50), channel_id=1, source_target_pairs={{0,2},{1,3},{2,0},{3,1},{4,6},{5,7},{6,4},{7,5},{8,10},{9,11},{10,... | collective-permute-start | bytes 1572872 | tf_op jit(solution)/shard_map/ppermute | solution.py:13
  236.1 26.9 %collective-permute-start.6 = (bf16[1024,2,128]{2,0,1:T(8,128)(2,1)}, bf16[1024,2,128]{2,0,1:T(8,128)(2,1)}, u32[]{:S(2)}, u32[]{:S(2)}) collective-permute-start(bf16[1024,2,128]{2,0,1:T(8,128)(2,1)} %copy.50), channel_id=1, source_target_pairs={{0,1},{1,0},{2,3},{3,2},{4,5},{5,4},{6,7},{7,6},{8,9},{9,8},{10,11... | collective-permute-start | bytes 1572872 | tf_op jit(solution)/shard_map/ppermute | solution.py:13
  330.3 27.8 %collective-permute-start.11 = (bf16[1024,2,128]{0,2,1:T(8,128)(2,1)S(1)}, bf16[1024,2,128]{0,2,1:T(8,128)(2,1)}, u32[]{:S(2)}, u32[]{:S(2)}) collective-permute-start(bf16[1024,2,128]{0,2,1:T(8,128)(2,1)S(1)} %fusion.26), channel_id=1, source_target_pairs={{0,4},{1,5},{2,6},{3,7},{4,0},{5,1},{6,2},{7,3},{8,12},{9,13},{10,... | collective-permute-start | bytes 1572872 | tf_op jit(solution)/shard_map/ppermute | solution.py:13
  334.1 27.3 %collective-permute-start.10 = (bf16[1024,2,128]{0,2,1:T(8,128)(2,1)}, bf16[1024,2,128]{0,2,1:T(8,128)(2,1)}, u32[]{:S(2)}, u32[]{:S(2)}) collective-permute-start(bf16[1024,2,128]{0,2,1:T(8,128)(2,1)} %fusion.25), channel_id=1, source_target_pairs={{0,2},{1,3},{2,0},{3,1},{4,6},{5,7},{6,4},{7,5},{8,10},{9,11},{10,... | collective-permute-start | bytes 1572872 | tf_op jit(solution)/shard_map/ppermute | solution.py:13
  337.5 23.8 %collective-permute-start.9 = (bf16[1024,2,128]{0,2,1:T(8,128)(2,1)}, bf16[1024,2,128]{0,2,1:T(8,128)(2,1)}, u32[]{:S(2)}, u32[]{:S(2)}) collective-permute-start(bf16[1024,2,128]{0,2,1:T(8,128)(2,1)} %fusion.24), channel_id=1, source_target_pairs={{0,1},{1,0},{2,3},{3,2},{4,5},{5,4},{6,7},{7,6},{8,9},{9,8},{10,11... | collective-permute-start | bytes 1572872 | tf_op jit(solution)/shard_map/ppermute | solution.py:13
  (12 other events, 56.8 us)
Sparse Core Ops, SparseCore 0:
  11.6 91.4 all-reduce.4
  132.5 88.4 all-reduce.6
  226.2 83.6 all-reduce.8
  340.1 79.2 all-reduce.10
Sparse Core Ops, SparseCore 1:
  14.2 20.7 all-gather.8
  36.4 18.0 all-gather.10
  134.5 17.2 all-gather.12
  228.4 17.2 all-gather.14
where the time goes:
time: 432 us; the launch traced here: 431 us
  waiting for transfers between devices  274 us (63%)
  matrix products  71.3 us (17%)
  between operations  25.3 us (6%)
  other arithmetic  21.8 us (5%)
  local copies, waits for them, and re-layouts  19.7 us (5%)
  starting transfers between devices  18.6 us (4%)
    psum x2, waiting for transfers between devices, per_device(): latent = lax.psum(partial_latent.astype(jnp.bfloat16), 'feat')  114 us
    psum x2, waiting for transfers between devices, per_device(): latent_back = lax.psum(partial_back.astype(jnp.bfloat16), 'feat')  112 us
    dot_general x20, matrix products, block_product(): jnp.einsum('tjd,jdh->tjh', left, right, preferred_element_type=jnp.float32)  53.9 us
    ppermute x12, waiting for transfers between devices, from_partner(): lax.ppermute(value, axis, [(i, i ^ 1 << distance) for i in range(lax.axis...  47.6 us
    convert_element_type x2, other arithmetic, per_device(): hidden = jax.nn.gelu(pre_act, approximate=False).astype(jnp.bfloat16)  20.7 us
    ppermute x12, starting transfers between devices, from_partner(): lax.ppermute(value, axis, [(i, i ^ 1 << distance) for i in range(lax.axis...  18.2 us
  transfers between devices with their start and end apart: 20, of which 9 were waited for; matrix products, arithmetic and copies ran while one was open for 24% of the time, Pallas kernels for 0%

commit v1 on v0

v1 whole, which is shorter than its diff:
```python
import functools
import math

import jax
import jax.numpy as jnp
from jax import lax
from jax.experimental import pallas as pl
from jax.experimental.pallas import tpu as pltpu
from jax.sharding import PartitionSpec as P

CHUNK_ROWS = 256
SKEW = 2
MESH = pl.DeviceIdType.MESH


def bits_of(count):
    return count.bit_length() - 1


def network(cfg, tokens, level_bits, up_in, down_in, rank_in, rank_up, rank_down, rank_out, out, *scratch):
    (xbuf, xrecv, tsend, trecv, part, half, full, hid, acc, wup, wdown) = scratch[:11]
    rest = scratch[11:]
    layers, rows, width = cfg["layers"], cfg["rows"], cfg["width"]
    blocks, wb, hb = cfg["blocks"], cfg["wb"], cfg["hb"]
    n_feat, n_tok, rank = cfg["n_feat"], cfg["n_tok"], cfg["rank"]
    cr = cfg["chunk"]
    chunks = rows // cr
    local_bits = bits_of(blocks)
    nb = bits_of(n_feat)
    levels = local_bits + nb
    gather = cfg["gather"]
    if gather:
        upg, downg = rest[:layers], rest[layers : 2 * layers]
        wsend, wrecv, wloc = rest[2 * layers : 2 * layers + 3]
        rest = rest[2 * layers + 3 :]
    else:
        upg = [up_in.at[l] for l in range(layers)]
        downg = [down_in.at[l] for l in range(layers)]
    xs_sem, xr_sem, ts_sem, tr_sem, as_sem, ar_sem = rest

    me = lax.axis_index("feat")
    me_tok = lax.axis_index("tok")
    mybit = [(me // (1 << b)) % 2 for b in range(nb)]
    partner = [me + (1 << b) * (1 - 2 * mybit[b]) for b in range(nb)]

    barrier = pltpu.get_barrier_semaphore()
    for b in range(nb):
        pl.semaphore_signal(barrier, inc=1, device_id={"feat": partner[b]}, device_id_type=MESH)
    greeted = nb
    if gather:
        for o in range(1, n_tok):
            pl.semaphore_signal(
                barrier, inc=1, device_id={"tok": lax.rem(me_tok + o, n_tok)}, device_id_type=MESH
            )
        greeted += n_tok - 1
    pl.semaphore_wait(barrier, greeted)

    def weight_copy(l, kind, o):
        if kind == 0:
            cols = up_in.shape[-1]
            src = up_in.at[l]
            dst = upg[l].at[:, :, :, pl.ds(pl.multiple_of(me_tok * cols, cols), cols)]
        else:
            cols = down_in.shape[-2]
            src = down_in.at[l]
            dst = downg[l].at[:, :, pl.ds(pl.multiple_of(me_tok * cols, cols), cols), :]
        if o == 0:
            return pltpu.make_async_copy(src, dst, wloc.at[l, kind])
        return pltpu.make_async_remote_copy(
            src_ref=src,
            dst_ref=dst,
            send_sem=wsend.at[l, kind, o - 1],
            recv_sem=wrecv.at[l, kind, o - 1],
            device_id={"tok": lax.rem(me_tok + o, n_tok)},
            device_id_type=MESH,
        )

    def start_weights():
        for l in range(layers):
            for kind in range(2):
                for o in range(n_tok):
                    weight_copy(l, kind, o).start()

    prepared = set()

    def prepare(l, kind):
        if (l, kind) in prepared:
            return
        prepared.add((l, kind))
        if gather:
            for o in range(n_tok):
                copy = weight_copy(l, kind, o)
                copy.wait() if o == 0 else copy.wait_recv()
        order = []
        for b in range(levels):
            at = 0
            for k in range(levels):
                at = jnp.maximum(at, jnp.where(level_bits[l, k] == b, 1 + k, 0))
            order.append(at)
        for j in range(blocks):
            if kind == 0:
                wup[l, j, pl.ds(0, wb), :] = upg[l][j, 0]
                for b in range(levels):
                    wup[l, j, pl.ds((1 + b) * wb, wb), :] = upg[l][j, order[b]]
                wup[l, j, pl.ds((1 + levels) * wb, rank), :] = rank_up[l, :, pl.ds(j * hb, hb)]
            else:
                wdown[l, j, pl.ds(0, wb), :] = downg[l][j, 0]
                for b in range(levels):
                    wdown[l, j, pl.ds((1 + b) * wb, wb), :] = downg[l][j, order[b]]

    def x_copy(l, c, b):
        at = pl.ds(c * cr, cr)
        return pltpu.make_async_remote_copy(
            src_ref=xbuf.at[l, at, :],
            dst_ref=xrecv.at[l, b, at, :],
            send_sem=xs_sem.at[l, c, b],
            recv_sem=xr_sem.at[l, c, b],
            device_id={"feat": partner[b]},
            device_id_type=MESH,
        )

    def t_copy(l, c, b):
        at = pl.ds(c * cr, cr)
        return pltpu.make_async_remote_copy(
            src_ref=tsend.at[l, b, at, :],
            dst_ref=trecv.at[l, b, at, :],
            send_sem=ts_sem.at[l, c, b],
            recv_sem=tr_sem.at[l, c, b],
            device_id={"feat": partner[b]},
            device_id_type=MESH,
        )

    last = nb - 1
    sizes = [cr >> (k + 1) for k in range(last)]
    own_at = [0]
    for k in range(last):
        own_at.append(own_at[-1] + mybit[k] * sizes[k])
    away_at = [own_at[k] + (1 - mybit[k]) * sizes[k] for k in range(last)]
    piece = cr >> last
    half_at = [sum(sizes[:k]) for k in range(last + 1)]
    half_rows = half_at[-1] + piece

    def reduce_copy(u, c, k):
        if k < last:
            src = part.at[u, pl.ds(pl.multiple_of(c * cr + away_at[k], sizes[k]), sizes[k]), :]
            size = sizes[k]
        else:
            src = part.at[u, pl.ds(pl.multiple_of(c * cr + own_at[last], piece), piece), :]
            size = piece
        return pltpu.make_async_remote_copy(
            src_ref=src,
            dst_ref=half.at[u, pl.ds(c * half_rows + half_at[k], size), :],
            send_sem=as_sem.at[u, c, k],
            recv_sem=ar_sem.at[u, c, k],
            device_id={"feat": partner[k]},
            device_id_type=MESH,
        )

    def spread_copy(u, c, k):
        size = cr >> (k + 1)
        at = pl.ds(pl.multiple_of(c * cr + own_at[k + 1], size), size)
        return pltpu.make_async_remote_copy(
            src_ref=full.at[u, at, :],
            dst_ref=full.at[u, at, :],
            send_sem=as_sem.at[u, c, nb + k],
            recv_sem=ar_sem.at[u, c, nb + k],
            device_id={"feat": partner[k]},
            device_id_type=MESH,
        )

    def sum_stage(u, c, k):
        reduce_copy(u, c, k).wait_recv()
        size = sizes[k] if k < last else piece
        start = own_at[k + 1] if k < last else own_at[last]
        at = pl.ds(pl.multiple_of(c * cr + start, size), size)
        total = part[u, at, :].astype(jnp.float32) + half[
            u, pl.ds(c * half_rows + half_at[k], size), :
        ].astype(jnp.float32)
        if k < last:
            part[u, at, :] = total.astype(jnp.bfloat16)
            reduce_copy(u, c, k + 1).start()
        else:
            full[u, at, :] = total.astype(jnp.bfloat16)
            if last > 0:
                spread_copy(u, c, last - 1).start()

    def spread_stage(u, c, k):
        spread_copy(u, c, k).wait_recv()
        if k > 0:
            spread_copy(u, c, k - 1).start()

    def sum_stages(u, c):
        found = [functools.partial(sum_stage, u, c, k) for k in range(nb)]
        for k in range(last - 1, 0, -1):
            found.append(functools.partial(spread_stage, u, c, k))
        return found

    def finish_sum(u, c):
        if last > 0:
            spread_stage(u, c, 0)

    def begin(l, c):
        at = pl.ds(c * cr, cr)
        u = 2 * l
        x = xbuf[l, at, :]
        mine = rank_in[l, pl.ds(pl.multiple_of(me * width, width), width), :]
        part[u, at, :] = jnp.dot(x, mine, preferred_element_type=jnp.float32).astype(jnp.bfloat16)
        reduce_copy(u, c, 0).start()
        for b in reversed(range(nb)):
            x_copy(l, c, b).start()

    def first(c):
        at = pl.ds(c * cr, cr)
        xbuf[0, at, :] = tokens[at, :]
        begin(0, c)

    def middle(l, c):
        at = pl.ds(c * cr, cr)
        u = 2 * l + 1
        prepare(l, 0)
        finish_sum(u - 1, c)
        for b in range(nb):
            x_copy(l, c, b).wait_recv()
        for j in range(blocks):
            pieces = [xbuf[l, at, pl.ds(j * wb, wb)]]
            for b in range(local_bits):
                pieces.append(xbuf[l, at, pl.ds((j ^ (1 << b)) * wb, wb)])
            for b in range(nb):
                pieces.append(xrecv[l, b, at, pl.ds(j * wb, wb)])
            pieces.append(full[u - 1, at, :])
            pre = jnp.dot(
                jnp.concatenate(pieces, axis=1), wup[l, j], preferred_element_type=jnp.float32
            )
            act = 0.5 * pre * (1.0 + lax.erf(pre * (1.0 / math.sqrt(2.0))))
            hid[at, pl.ds(j * hb, hb)] = act.astype(jnp.bfloat16)
        part[u, at, :] = jnp.dot(
            hid[at, :], rank_down[l], preferred_element_type=jnp.float32
        ).astype(jnp.bfloat16)
        reduce_copy(u, c, 0).start()
        prepare(l, 1)
        own = [None] * blocks
        for j in range(blocks):
            out_j = lax.dot_general(
                hid[at, pl.ds(j * hb, hb)],
                wdown[l, j],
                (((1,), (1,)), ((), ())),
                preferred_element_type=jnp.float32,
            )
            terms = [out_j[:, k * wb : (k + 1) * wb] for k in range(1 + levels)]
            for b in range(nb):
                tsend[l, b, at, pl.ds(j * wb, wb)] = terms[1 + local_bits + b].astype(jnp.bfloat16)
            for to, value in [(j, terms[0])] + [(j ^ (1 << b), terms[1 + b]) for b in range(local_bits)]:
                own[to] = value if own[to] is None else own[to] + value
        for b in reversed(range(nb)):
            t_copy(l, c, b).start()
        for j in range(blocks):
            col = pl.ds(j * wb, wb)
            acc[at, col] = own[j] + xbuf[l, at, col].astype(jnp.float32)

    def close(l, c):
        at = pl.ds(c * cr, cr)
        u = 2 * l + 1
        finish_sum(u, c)
        total = acc[at, :] + jnp.dot(full[u, at, :], rank_out[l], preferred_element_type=jnp.float32)
        for b in range(nb):
            t_copy(l, c, b).wait_recv()
            total = total + trecv[l, b, at, :].astype(jnp.float32)
        result = total.astype(jnp.bfloat16)
        if l + 1 < layers:
            xbuf[l + 1, at, :] = result
            begin(l + 1, c)
        else:
            out[at, :] = result

    plan = []
    for c in range(chunks):
        steps = [functools.partial(first, c)]
        for l in range(layers):
            steps += sum_stages(2 * l, c)
            steps.append(functools.partial(middle, l, c))
            steps += sum_stages(2 * l + 1, c)
            steps.append(functools.partial(close, l, c))
        plan.append(steps)

    plan[0][0]()
    if gather:
        start_weights()
    for tick in range(1, len(plan[0]) + cfg["skew"] * (chunks - 1)):
        for c in range(chunks):
            at = tick - cfg["skew"] * c
            if 0 <= at < len(plan[c]):
                plan[c][at]()

    for l in range(layers):
        if gather:
            for kind in range(2):
                for o in range(1, n_tok):
                    weight_copy(l, kind, o).wait_send()
        for c in range(chunks):
            for b in range(nb):
                x_copy(l, c, b).wait_send()
                t_copy(l, c, b).wait_send()
            for u in (2 * l, 2 * l + 1):
                for k in range(nb):
                    reduce_copy(u, c, k).wait_send()
                for k in range(last):
                    spread_copy(u, c, k).wait_send()


def per_device(tokens, level_bits, up_blocks, down_blocks, rank_in, rank_up, rank_down, rank_out):
    rows, width = tokens.shape
    layers, blocks, parts, wb, up_cols = up_blocks.shape
    hb, down_cols = down_blocks.shape[3:]
    n_tok, n_feat = lax.axis_size("tok"), lax.axis_size("feat")
    rank = rank_in.shape[-1]
    hidden = blocks * hb
    nb = bits_of(n_feat)
    chunk = min(CHUNK_ROWS, rows)
    chunks = rows // chunk
    gather = n_tok > 1 and up_cols % 128 == 0 and down_cols % 16 == 0
    if not gather:
        up_blocks = lax.all_gather(up_blocks, "tok", axis=4, tiled=True)
        down_blocks = lax.all_gather(down_blocks, "tok", axis=4, tiled=True)
    down_blocks = jnp.swapaxes(down_blocks, 3, 4)
    cfg = dict(
        layers=layers, rows=rows, width=width, blocks=blocks, wb=wb, hb=hb, n_feat=n_feat,
        n_tok=n_tok, rank=rank, chunk=chunk, gather=gather, skew=SKEW,
    )
    bf16 = jnp.bfloat16
    uses = 2 * layers
    half_rows = chunk
    scratch = [
        pltpu.VMEM((layers, rows, width), bf16),
        pltpu.VMEM((layers, nb, rows, width), bf16),
        pltpu.VMEM((layers, nb, rows, width), bf16),
        pltpu.VMEM((layers, nb, rows, width), bf16),
        pltpu.VMEM((uses, rows, rank), bf16),
        pltpu.VMEM((uses, chunks * half_rows, rank), bf16),
        pltpu.VMEM((uses, rows, rank), bf16),
        pltpu.VMEM((rows, hidden), bf16),
        pltpu.VMEM((rows, width), jnp.float32),
        pltpu.VMEM((layers, blocks, parts * wb + rank, hb), bf16),
        pltpu.VMEM((layers, blocks, parts * wb, hb), bf16),
    ]
    dma = pltpu.SemaphoreType.DMA
    if gather:
        scratch += [pltpu.VMEM((blocks, parts, wb, hb), bf16)] * (2 * layers)
        scratch += [
            dma((layers, 2, n_tok - 1)),
            dma((layers, 2, n_tok - 1)),
            dma((layers, 2)),
        ]
    scratch += [dma((layers, chunks, nb))] * 4 + [dma((uses, chunks, 2 * nb - 1))] * 2
    vmem = pl.BlockSpec(memory_space=pltpu.VMEM)
    smem = pl.BlockSpec(memory_space=pltpu.SMEM)
    return pl.pallas_call(
        functools.partial(network, cfg),
        out_shape=jax.ShapeDtypeStruct((rows, width), bf16),
        in_specs=[vmem, smem] + [vmem] * 6,
        out_specs=vmem,
        scratch_shapes=scratch,
        compiler_params=pltpu.CompilerParams(
            collective_id=0, has_side_effects=True, vmem_limit_bytes=63 * 1024 * 1024
        ),
    )(tokens, level_bits, up_blocks, down_blocks, rank_in, rank_up, rank_down, rank_out)


def solution(mesh):
    return jax.shard_map(
        per_device,
        mesh=mesh,
        in_specs=(
            P("tok", "feat"),
            P(),
            P(None, "feat", None, None, "tok"),
            P(None, "feat", None, None, "tok"),
            P(),
            P(None, None, "feat"),
            P(None, "feat", None),
            P(None, None, "feat"),
        ),
        out_specs=P("tok", "feat"),
        check_vma=False,
    )
```

time: 432 us -> 162 us (0.38)
  waiting for transfers between devices: 274 us -> 0 us
  Pallas kernels: 0 us -> 159 us
  matrix products: 71.3 us -> 0 us
  between operations: 25.3 us -> 0.01 us
  other arithmetic: 21.8 us -> 0 us
  starting transfers between devices: 18.6 us -> 0 us
  local copies, waits for them, and re-layouts: 19.7 us -> 1.87 us
    psum x4 -> x0, waiting for transfers between devices: 226 us -> none  [the longest x2 114 us: per_device(): latent = lax.psum(partial_latent.astype(jnp.bfloat16), 'feat')]
    pallas_call x0 -> x1, Pallas kernels: none -> 159 us  [per_device(): pl.pallas_call(functools.partial(network, cfg), out_shape=jax.ShapeDtypeS...]
    dot_general x28 -> x0, matrix products: 71.3 us -> none  [the longest x20 53.9 us: block_product(): jnp.einsum('tjd,jdh->tjh', left, right, preferred_element_type=jnp.float32)]
    ppermute x12 -> x0, waiting for transfers between devices: 47.6 us -> none  [from_partner(): lax.ppermute(value, axis, [(i, i ^ 1 << distance) for i in range(lax.axis...]
    convert_element_type x4 -> x0, other arithmetic: 20.9 us -> none  [the longest x2 20.7 us: per_device(): hidden = jax.nn.gelu(pre_act, approximate=False).astype(jnp.bfloat16)]
    ppermute x12 -> x0, starting transfers between devices: 18.2 us -> none  [from_partner(): lax.ppermute(value, axis, [(i, i ^ 1 << distance) for i in range(lax.axis...]
    slice x3 -> x0, local copies, waits for them, and re-layouts: 6.53 us -> none  [the longest x1 2.71 us: per_device(): rank_in[layer_num]]
    reshape x4 -> x0, local copies, waits for them, and re-layouts: 5.37 us -> none  [the longest x2 3.36 us: flip_pairs(): return jnp.flip(array.reshape(split), axis + 1).reshape(shape)]
  transfers between devices with their start and end apart: 20 -> 0, of which waited for: 9 -> 0; matrix products, arithmetic and copies ran while one was open for 24% -> 0% of each run, Pallas kernels for 0% -> 0%
where the time goes in v1:
time: 162 us; the launch traced here: 161 us
  Pallas kernels  159 us (98%)
  local copies, waits for them, and re-layouts  1.87 us (1%)
    pallas_call x1, Pallas kernels, per_device(): pl.pallas_call(functools.partial(network, cfg), out_shape=jax.ShapeDtypeS...  159 us

profile of v1, /device:TPU:0, one launch (start us, length us, event | category | flops | bytes accessed | tf_op | source)
XLA Modules:
  0.0 161.2 jit_solution(4480460906990258100)
XLA Ops:
  0.0 159.3 %shard_map.82 = bf16[1024,256]{1,0:T(8,128)(2,1)} custom-call(bf16[1024,256]{1,0:T(8,128)(2,1)} %tokens.1, s32[2,4]{1,0:T(2,128)} %level_bits.1, bf16[2,2,5,128,128]{4,3,2,1,0:T(8,128)(2,1)} %up_in.1, bf16[2,2,5,32,512]{4,3,2,1,0:T(8,128)(2,1)} %bitcast.1, bf16[2,2048,256]{2,1,0:T(8,128)(2,1)} %rank_in.1, bf16[2,256,1024]{2,1,0:T(8,128)(2,1)} %rank_up.1, ...), custom_call_target="tpu_custom_call" | custom-call | tf_op jit(solution)/shard_map/pallas_call | solution.py:356
  159.3 1.9 %copy.10 = bf16[1024,256]{1,0:T(8,128)(2,1)} copy(bf16[1024,256]{1,0:T(8,128)(2,1)} %shard_map.82) | data formatting | bytes 1048576

commit v2 on v1

--- a/solution.py
+++ b/solution.py
@@ -9,7 +9,8 @@
 from jax.sharding import PartitionSpec as P
 
 CHUNK_ROWS = 256
-SKEW = 2
+SKEW = 1
+LATER = 1
 MESH = pl.DeviceIdType.MESH
 
 
@@ -168,6 +169,11 @@
             device_id_type=MESH,
         )
 
+    def start_bulk(u, c, stage):
+        for b in reversed(range(nb)):
+            if min(LATER, nb) * (0 if b == last else 1) == stage:
+                (t_copy if u % 2 else x_copy)(u // 2, c, b).start()
+
     def sum_stage(u, c, k):
         reduce_copy(u, c, k).wait_recv()
         size = sizes[k] if k < last else piece
@@ -183,6 +189,7 @@
             full[u, at, :] = total.astype(jnp.bfloat16)
             if last > 0:
                 spread_copy(u, c, last - 1).start()
+        start_bulk(u, c, k + 1)
 
     def spread_stage(u, c, k):
         spread_copy(u, c, k).wait_recv()
@@ -206,8 +213,7 @@
         mine = rank_in[l, pl.ds(pl.multiple_of(me * width, width), width), :]
         part[u, at, :] = jnp.dot(x, mine, preferred_element_type=jnp.float32).astype(jnp.bfloat16)
         reduce_copy(u, c, 0).start()
-        for b in reversed(range(nb)):
-            x_copy(l, c, b).start()
+        start_bulk(u, c, 0)
 
     def first(c):
         at = pl.ds(c * cr, cr)
@@ -251,8 +257,7 @@
                 tsend[l, b, at, pl.ds(j * wb, wb)] = terms[1 + local_bits + b].astype(jnp.bfloat16)
             for to, value in [(j, terms[0])] + [(j ^ (1 << b), terms[1 + b]) for b in range(local_bits)]:
                 own[to] = value if own[to] is None else own[to] + value
-        for b in reversed(range(nb)):
-            t_copy(l, c, b).start()
+        start_bulk(u, c, 0)
         for j in range(blocks):
             col = pl.ds(j * wb, wb)
             acc[at, col] = own[j] + xbuf[l, at, col].astype(jnp.float32)

time: 162 us -> 147 us (0.907)
  Pallas kernels: 159 us -> 144 us
    pallas_call x1, Pallas kernels: 159 us -> 144 us  [per_device(): pl.pallas_call(functools.partial(network, cfg), out_shape=jax.ShapeDtypeS...]
where the time goes in v2:
time: 147 us; the launch traced here: 146 us
  Pallas kernels  144 us (98%)
  local copies, waits for them, and re-layouts  1.87 us (1%)
    pallas_call x1, Pallas kernels, per_device(): pl.pallas_call(functools.partial(network, cfg), out_shape=jax.ShapeDtypeS...  144 us

profile of v2, /device:TPU:0, one launch (start us, length us, event | category | flops | bytes accessed | tf_op | source)
XLA Modules:
  0.0 146.3 jit_solution(15288670204581476173)
XLA Ops:
  0.0 144.5 %shard_map.82 = bf16[1024,256]{1,0:T(8,128)(2,1)} custom-call(bf16[1024,256]{1,0:T(8,128)(2,1)} %tokens.1, s32[2,4]{1,0:T(2,128)} %level_bits.1, bf16[2,2,5,128,128]{4,3,2,1,0:T(8,128)(2,1)} %up_in.1, bf16[2,2,5,32,512]{4,3,2,1,0:T(8,128)(2,1)} %bitcast.1, bf16[2,2048,256]{2,1,0:T(8,128)(2,1)} %rank_in.1, bf16[2,256,1024]{2,1,0:T(8,128)(2,1)} %rank_up.1, ...), custom_call_target="tpu_custom_call" | custom-call | tf_op jit(solution)/shard_map/pallas_call | solution.py:361
  144.5 1.9 %copy.10 = bf16[1024,256]{1,0:T(8,128)(2,1)} copy(bf16[1024,256]{1,0:T(8,128)(2,1)} %shard_map.82) | data formatting | bytes 1048576
